TPU v7x, 128 devices: a whole 4x4x4 slice. The times are simulated.
128 devices in a mesh: shard: 16 (over z, x), context: 4 (over y), tensor: 2 (over core).
Axes of the slice: x: 4, y: 4, z: 4, core: 2. Of those that a mesh axis runs over, the one named last changes fastest.
Arguments:
- inputs: float32 [32, 512, 768], P('shard', 'context'), may hold values from -6 to 6
- segment_ids: int32 [32, 512], P('shard', 'context'), may hold values from 0 to 3, never falling along the last dimension, each value on 1 to 256 neighbouring positions
- projection: bfloat16 [2, 3, 768, 768], P(None, None, 'shard', 'tensor'), may hold values from -1 to 1
- head_bias: bfloat16 [2, 2, 12, 64], P(None, None, 'tensor', 'shard'), may hold values from -3 to 3
- mixing: bfloat16 [2, 768, 768], P(None, 'tensor', 'shard'), may hold values from -0.875 to 0.875
- expansion: bfloat16 [2, 768, 3072], P(None, 'shard', 'tensor'), may hold values from -0.21875 to 0.21875
- hidden_bias: bfloat16 [2, 48, 64], P(None, 'tensor', 'shard'), may hold values from -3 to 3
- contraction: bfloat16 [2, 3072, 768], P(None, 'tensor', 'shard'), may hold values from -0.109375 to 0.109375
- norm_gains: bfloat16 [2, 2, 768], P(None, None, 'shard'), may hold values from 0.3984375 to 1.59375
- offsets: bfloat16 [2, 4, 768], P(None, None, 'shard'), may hold values from -2 to 2
- cotangent: float32 [32, 512, 768], P('shard', 'context'), may hold values from -6 to 6
Outputs:
- outputs: float32 [32, 512, 768], P('shard', 'context')
- input_grad: float32 [32, 512, 768], P('shard', 'context')
- grad_projection: float32 [2, 3, 768, 768], P(None, None, 'shard', 'tensor')
- head_grad: float32 [2, 2, 12, 64], P(None, None, 'tensor', 'shard')
- grad_mixing: float32 [2, 768, 768], P(None, 'tensor', 'shard')
- grad_expansion: float32 [2, 768, 3072], P(None, 'shard', 'tensor')
- hidden_grad: float32 [2, 48, 64], P(None, 'tensor', 'shard')
- grad_contraction: float32 [2, 3072, 768], P(None, 'tensor', 'shard')
- gains_grad: float32 [2, 2, 768], P(None, None, 'shard')
- grad_offsets: float32 [2, 4, 768], P(None, None, 'shard')
Inputs may be any that keep to these rules, and one draw needn't show every extreme that they name: `segment_ids`: within a row ids never fall; every document holds 1 to 256 positions and in every row some document holds exactly 256.
All inputs are finite; a program needn't handle non-finite values.
Results may differ from a plain program's by a relative error of at most 0.033.
Values may be sent and summed in bfloat16 or wider, within the bound.
No kernel may reach another device: no remote copies, remote signals or barrier semaphores. Data moves between devices by JAX's collectives and lax.ppermute only.
A program may use at most 128 MiB of HBM per device.

v0:
```python
import jax
import jax.numpy as jnp
from jax import lax
from jax.sharding import PartitionSpec as P

HEAD = 64
EPS = 1e-05
GELU_COEF = 0.7978845608028654
GELU_CUBE = 0.044715
MASKED = -1e30


def gelu_value(preact):
    inner_arg = GELU_COEF * (preact + GELU_CUBE * preact * preact * preact)
    return 0.5 * preact * (1.0 + jnp.tanh(inner_arg))


def gelu_slope(preact):
    inner_arg = GELU_COEF * (preact + GELU_CUBE * preact * preact * preact)
    tanh_value = jnp.tanh(inner_arg)
    return 0.5 * (1.0 + tanh_value) + 0.5 * preact * (1.0 - tanh_value * tanh_value) * GELU_COEF * (
        1.0 + 3.0 * GELU_CUBE * preact * preact
    )


def norm_forward(stream):
    center = stream - jnp.mean(stream, axis=-1, keepdims=True)
    spread = lax.rsqrt(jnp.mean(center * center, axis=-1, keepdims=True) + EPS)
    return (center * spread, spread)


def norm_backward(upstream, normed, spread, gain_row):
    scaled = upstream * gain_row
    first_mean = jnp.mean(scaled, axis=-1, keepdims=True)
    second_mean = jnp.mean(scaled * normed, axis=-1, keepdims=True)
    return spread * (scaled - first_mean - normed * second_mean)


def masked_scores(query_block, key_block, visible, head_scale):
    scores = (
        jnp.einsum("rqhe,rkhe->rhqk", query_block, key_block, preferred_element_type=jnp.float32)
        * head_scale
    )
    return jnp.where(visible, scores, MASKED)


def per_device(
    inputs,
    segment_ids,
    projection,
    head_bias,
    mixing,
    expansion,
    hidden_bias,
    contraction,
    norm_gains,
    offsets,
    cotangent,
):
    layers = projection.shape[0]
    row_count, block_length, model_width = inputs.shape
    context_size = lax.axis_size("context")
    heads_here = head_bias.shape[2]
    head_scale = HEAD ** (-0.5)
    segment_half = segment_ids.astype(jnp.bfloat16)
    query_pos = lax.axis_index("context") * block_length + jnp.arange(block_length, dtype=jnp.int32)
    key_pos = jnp.arange(block_length * context_size, dtype=jnp.int32)
    stream = inputs
    kept_state = []
    for layer_index in range(layers):
        weights = (
            lax.all_gather(projection[layer_index], "shard", axis=1, tiled=True),
            lax.all_gather(head_bias[layer_index], "shard", axis=2, tiled=True),
            lax.all_gather(mixing[layer_index], "shard", axis=1, tiled=True),
            lax.all_gather(expansion[layer_index], "shard", axis=0, tiled=True),
            lax.all_gather(hidden_bias[layer_index], "shard", axis=1, tiled=True),
            lax.all_gather(contraction[layer_index], "shard", axis=1, tiled=True),
            lax.all_gather(norm_gains[layer_index], "shard", axis=1, tiled=True),
            lax.all_gather(offsets[layer_index], "shard", axis=1, tiled=True),
        )
        (
            qkv_weight,
            qkv_bias,
            out_weight,
            up_weight,
            up_bias,
            down_weight,
            gain_rows,
            offset_rows,
        ) = weights
        gain_float = gain_rows.astype(jnp.float32)
        offset_float = offset_rows.astype(jnp.float32)
        normed_one, spread_one = norm_forward(stream)
        attend_input = (normed_one * gain_float[0] + offset_float[0]).astype(jnp.bfloat16)
        projected = jnp.einsum(
            "rtd,jdc->jrtc", attend_input, qkv_weight, preferred_element_type=jnp.float32
        )
        bias_float = qkv_bias.astype(jnp.float32).reshape(2, -1)
        query_rows = (projected[0] + bias_float[0]).astype(jnp.bfloat16)
        key_rows = projected[1].astype(jnp.bfloat16)
        value_rows = (projected[2] + bias_float[1]).astype(jnp.bfloat16)
        keys_all, values_all, segments_all = (
            lax.all_gather(key_rows, "context", axis=1, tiled=True),
            lax.all_gather(value_rows, "context", axis=1, tiled=True),
            lax.all_gather(segment_half, "context", axis=1, tiled=True),
        )
        visible = (segments_all[:, None, :] == segment_half[:, :, None]) & (
            key_pos[None, None, :] <= query_pos[None, :, None]
        )
        visible = visible[:, None]
        query_block = query_rows.reshape(row_count, block_length, heads_here, HEAD)
        key_block = keys_all.reshape(row_count, -1, heads_here, HEAD)
        value_block = values_all.reshape(row_count, -1, heads_here, HEAD)
        masked = masked_scores(query_block, key_block, visible, head_scale)
        row_top = jnp.max(masked, axis=-1, keepdims=True)
        log_total = row_top + jnp.log(jnp.sum(jnp.exp(masked - row_top), axis=-1, keepdims=True))
        soft_half = jnp.exp(masked - log_total).astype(jnp.bfloat16)
        attended = (
            jnp.einsum(
                "rhqk,rkhe->rqhe", soft_half, value_block, preferred_element_type=jnp.float32
            )
            .astype(jnp.bfloat16)
            .reshape(row_count, block_length, -1)
        )
        attend_part = jnp.einsum(
            "rtc,cd->rtd", attended, out_weight, preferred_element_type=jnp.float32
        )
        middle = stream + lax.psum(attend_part, "tensor") + offset_float[2]
        normed_two, spread_two = norm_forward(middle)
        feed_input = (normed_two * gain_float[1] + offset_float[1]).astype(jnp.bfloat16)
        preact = jnp.einsum(
            "rtd,df->rtf", feed_input, up_weight, preferred_element_type=jnp.float32
        ) + up_bias.astype(jnp.float32).reshape(-1)
        activation = gelu_value(preact).astype(jnp.bfloat16)
        feed_part = jnp.einsum(
            "rtf,fd->rtd", activation, down_weight, preferred_element_type=jnp.float32
        )
        stream = middle + lax.psum(feed_part, "tensor") + offset_float[3]
        stored = ()
        kept_state.append(
            (
                stored,
                normed_one,
                spread_one,
                attend_input,
                query_block,
                key_block,
                value_block,
                visible,
                log_total,
                attended,
                normed_two,
                spread_two,
                feed_input,
                preact,
                activation,
            )
        )
    upstream = cotangent
    collected = []
    for layer_index in reversed(range(layers)):
        (
            stored,
            normed_one,
            spread_one,
            attend_input,
            query_block,
            key_block,
            value_block,
            visible,
            log_total,
            attended,
            normed_two,
            spread_two,
            feed_input,
            preact,
            activation,
        ) = kept_state[layer_index]
        current = (
            lax.all_gather(projection[layer_index], "shard", axis=1, tiled=True),
            lax.all_gather(head_bias[layer_index], "shard", axis=2, tiled=True),
            lax.all_gather(mixing[layer_index], "shard", axis=1, tiled=True),
            lax.all_gather(expansion[layer_index], "shard", axis=0, tiled=True),
            lax.all_gather(hidden_bias[layer_index], "shard", axis=1, tiled=True),
            lax.all_gather(contraction[layer_index], "shard", axis=1, tiled=True),
            lax.all_gather(norm_gains[layer_index], "shard", axis=1, tiled=True),
            lax.all_gather(offsets[layer_index], "shard", axis=1, tiled=True),
        )
        (
            qkv_weight,
            qkv_bias,
            out_weight,
            up_weight,
            up_bias,
            down_weight,
            gain_rows,
            offset_rows,
        ) = current
        gain_float = gain_rows.astype(jnp.float32)
        upstream_half = upstream.astype(jnp.bfloat16)
        contraction_part = jnp.einsum(
            "rtf,rtd->fd", activation, upstream_half, preferred_element_type=jnp.float32
        )
        offset_down = jnp.sum(upstream, axis=(0, 1))
        hidden_back = jnp.einsum(
            "rtd,fd->rtf", upstream_half, down_weight, preferred_element_type=jnp.float32
        ) * gelu_slope(preact)
        hidden_half = hidden_back.astype(jnp.bfloat16)
        hidden_part = jnp.sum(hidden_back, axis=(0, 1)).reshape(up_bias.shape)
        expansion_part = jnp.einsum(
            "rtd,rtf->df", feed_input, hidden_half, preferred_element_type=jnp.float32
        )
        feed_partial = jnp.einsum(
            "rtf,df->rtd", hidden_half, up_weight, preferred_element_type=jnp.float32
        )
        feed_back = lax.psum(feed_partial.astype(jnp.bfloat16), "tensor").astype(jnp.float32)
        gain_two = jnp.sum(feed_back * normed_two, axis=(0, 1))
        offset_two = jnp.sum(feed_back, axis=(0, 1))
        middle_back = upstream + norm_backward(feed_back, normed_two, spread_two, gain_float[1])
        middle_half = middle_back.astype(jnp.bfloat16)
        mixing_part = jnp.einsum(
            "rtc,rtd->cd", attended, middle_half, preferred_element_type=jnp.float32
        )
        offset_mix = jnp.sum(middle_back, axis=(0, 1))
        attended_back = jnp.einsum(
            "rtd,cd->rtc", middle_half, out_weight, preferred_element_type=jnp.float32
        ).astype(jnp.bfloat16)
        back_heads = attended_back.reshape(row_count, block_length, heads_here, HEAD)
        attended_heads = attended.reshape(row_count, block_length, heads_here, HEAD)
        row_delta = jnp.sum(
            back_heads.astype(jnp.float32) * attended_heads.astype(jnp.float32), axis=-1
        )
        masked = masked_scores(query_block, key_block, visible, head_scale)
        soft = jnp.exp(masked - log_total)
        soft_half = soft.astype(jnp.bfloat16)
        prob_back = jnp.einsum(
            "rqhe,rkhe->rhqk", back_heads, value_block, preferred_element_type=jnp.float32
        )
        score_back = (
            soft * (prob_back - jnp.transpose(row_delta, (0, 2, 1))[..., None]) * head_scale
        ).astype(jnp.bfloat16)
        query_back = jnp.einsum(
            "rhqk,rkhe->rqhe", score_back, key_block, preferred_element_type=jnp.float32
        ).reshape(row_count, block_length, -1)
        key_full = jnp.einsum(
            "rhqk,rqhe->rkhe", score_back, query_block, preferred_element_type=jnp.float32
        ).reshape(row_count, block_length * context_size, -1)
        value_full = jnp.einsum(
            "rhqk,rqhe->rkhe", soft_half, back_heads, preferred_element_type=jnp.float32
        ).reshape(row_count, block_length * context_size, -1)
        key_back, value_back = (
            lax.psum_scatter(
                key_full.astype(jnp.bfloat16), "context", scatter_dimension=1, tiled=True
            ).astype(jnp.float32),
            lax.psum_scatter(
                value_full.astype(jnp.bfloat16), "context", scatter_dimension=1, tiled=True
            ).astype(jnp.float32),
        )
        head_part = jnp.stack(
            [jnp.sum(query_back, axis=(0, 1)), jnp.sum(value_back, axis=(0, 1))]
        ).reshape(qkv_bias.shape)
        project_back = jnp.stack([query_back, key_back, value_back]).astype(jnp.bfloat16)
        projection_part = jnp.einsum(
            "rtd,jrtc->jdc", attend_input, project_back, preferred_element_type=jnp.float32
        )
        input_partial = jnp.einsum(
            "jrtc,jdc->rtd", project_back, qkv_weight, preferred_element_type=jnp.float32
        )
        input_back = lax.psum(input_partial.astype(jnp.bfloat16), "tensor").astype(jnp.float32)
        gain_one = jnp.sum(input_back * normed_one, axis=(0, 1))
        offset_one = jnp.sum(input_back, axis=(0, 1))
        upstream = middle_back + norm_backward(input_back, normed_one, spread_one, gain_float[0])
        grad_parts = (
            projection_part,
            head_part,
            mixing_part,
            expansion_part,
            hidden_part,
            contraction_part,
            jnp.stack([gain_one, gain_two]),
            jnp.stack([offset_one, offset_two, offset_mix, offset_down]),
        )
        collected.insert(
            0,
            (
                lax.psum(
                    lax.psum_scatter(
                        grad_parts[0].astype(jnp.bfloat16), "shard", scatter_dimension=1, tiled=True
                    ),
                    "context",
                ).astype(jnp.float32),
                lax.psum(
                    lax.psum_scatter(
                        grad_parts[1].astype(jnp.bfloat16), "shard", scatter_dimension=2, tiled=True
                    ),
                    "context",
                ).astype(jnp.float32),
                lax.psum(
                    lax.psum_scatter(
                        grad_parts[2].astype(jnp.bfloat16), "shard", scatter_dimension=1, tiled=True
                    ),
                    "context",
                ).astype(jnp.float32),
                lax.psum(
                    lax.psum_scatter(
                        grad_parts[3].astype(jnp.bfloat16), "shard", scatter_dimension=0, tiled=True
                    ),
                    "context",
                ).astype(jnp.float32),
                lax.psum(
                    lax.psum_scatter(
                        grad_parts[4].astype(jnp.bfloat16), "shard", scatter_dimension=1, tiled=True
                    ),
                    "context",
                ).astype(jnp.float32),
                lax.psum(
                    lax.psum_scatter(
                        grad_parts[5].astype(jnp.bfloat16), "shard", scatter_dimension=1, tiled=True
                    ),
                    "context",
                ).astype(jnp.float32),
                lax.psum(
                    lax.psum_scatter(
                        grad_parts[6].astype(jnp.bfloat16), "shard", scatter_dimension=1, tiled=True
                    ),
                    "context",
                ).astype(jnp.float32),
                lax.psum(
                    lax.psum_scatter(
                        grad_parts[7].astype(jnp.bfloat16), "shard", scatter_dimension=1, tiled=True
                    ),
                    "context",
                ).astype(jnp.float32),
            ),
        )
    stacked = [jnp.stack([entry[member] for entry in collected]) for member in range(8)]
    return (
        stream,
        upstream,
        stacked[0],
        stacked[1],
        stacked[2],
        stacked[3],
        stacked[4],
        stacked[5],
        stacked[6],
        stacked[7],
    )


def solution(mesh):
    in_specs = (
        P("shard", "context", None),
        P("shard", "context"),
        P(None, None, "shard", "tensor"),
        P(None, None, "tensor", "shard"),
        P(None, "tensor", "shard"),
        P(None, "shard", "tensor"),
        P(None, "tensor", "shard"),
        P(None, "tensor", "shard"),
        P(None, None, "shard"),
        P(None, None, "shard"),
        P("shard", "context", None),
    )
    out_specs = (
        P("shard", "context", None),
        P("shard", "context", None),
        P(None, None, "shard", "tensor"),
        P(None, None, "tensor", "shard"),
        P(None, "tensor", "shard"),
        P(None, "shard", "tensor"),
        P(None, "tensor", "shard"),
        P(None, "tensor", "shard"),
        P(None, None, "shard"),
        P(None, None, "shard"),
    )
    return jax.shard_map(
        per_device, mesh=mesh, in_specs=in_specs, out_specs=out_specs, check_vma=False
    )
```

profile of v0, /device:TPU:0, one launch (start us, length us, event | category | flops | bytes accessed | tf_op | source)
XLA Modules:
  0.0 1538.7 jit_solution(7133893320823804238)
XLA Ops:
  10.4 25.5 %all-gather.1 = bf16[1,4,768]{1,0,2:T(2,128)(2,1)S(1)} all-gather(bf16[1,4,48]{1,0,2:T(2,128)(2,1)S(1)} %copy.288), channel_id=3, replica_groups=mesh['shard'=16,'context'=4,'tensor'=2] {'shard'}, dimensions={2}, use_global_device_ids=true | all-gather | bytes 6528 | tf_op jit(solution)/shard_map/all_gather | solution.py:79
  37.0 23.4 %all-gather = bf16[1,2,768]{1,0,2:T(2,128)(2,1)S(1)} all-gather(bf16[1,2,48]{1,0,2:T(2,128)(2,1)S(1)} %copy.287), channel_id=2, replica_groups=mesh['shard'=16,'context'=4,'tensor'=2] {'shard'}, dimensions={2}, use_global_device_ids=true | all-gather | bytes 3264 | tf_op jit(solution)/shard_map/all_gather | solution.py:78
  61.4 21.3 %all-gather.3 = bf16[1,2,6,64]{2,1,0,3:T(2,128)(2,1)S(1)} all-gather(bf16[1,2,6,4]{2,1,0,3:T(2,128)(2,1)S(1)} %copy.289), channel_id=5, replica_groups=mesh['shard'=16,'context'=4,'tensor'=2] {'shard'}, dimensions={3}, use_global_device_ids=true | all-gather | bytes 1632 | tf_op jit(solution)/shard_map/all_gather | solution.py:73
  83.1 10.0 all_gather.79
  93.1 23.9 %all-gather.5 = bf16[1,384,768]{1,2,0:T(8,128)(2,1)S(1)} all-gather(bf16[1,384,48]{1,2,0:T(8,128)(2,1)S(1)} %get-tuple-element.105), channel_id=7, replica_groups=mesh['shard'=16,'context'=4,'tensor'=2] {'shard'}, dimensions={2}, use_global_device_ids=true | all-gather | bytes 626688 | tf_op jit(solution)/shard_map/all_gather | solution.py:74
  117.2 4.6 slice_reduce_fusion.8
  122.1 11.0 slice_reduce_fusion.6
  136.3 14.4 all-gather.4
  157.9 13.3 all_gather.78
  171.6 3.1 convolution_convert_fusion.5
  178.3 21.3 %all-gather.7 = bf16[1,24,64]{1,0,2:T(2,128)(2,1)S(1)} all-gather(bf16[1,24,4]{1,0,2:T(2,128)(2,1)S(1)} %copy.290), channel_id=9, replica_groups=mesh['shard'=16,'context'=4,'tensor'=2] {'shard'}, dimensions={2}, use_global_device_ids=true | all-gather | bytes 3264 | tf_op jit(solution)/shard_map/all_gather | solution.py:76
  201.3 47.0 %all-gather.27.cloned.1.call-done = bf16[1,768,1536]{2,1,0:T(8,128)(2,1)} async-done(((bf16[1,48,1536]{2,1,0:T(8,128)(2,1)}), bf16[1,768,1536]{2,1,0:T(8,128)(2,1)}) %all-gather.27.cloned.1.call-update) | async-done | bytes 2359312 | tf_op jit(solution)/shard_map/all_gather | solution.py:75
  248.4 2.5 convolution_add_fusion.1
  250.9 45.3 %all-gather.29.cloned.1.call-done = bf16[1,1536,768]{1,2,0:T(8,128)(2,1)} async-done(((bf16[1,1536,48]{1,2,0:T(8,128)(2,1)}), bf16[1,1536,768]{1,2,0:T(8,128)(2,1)}) %all-gather.29.cloned.1.call-update) | async-done | bytes 2359312 | tf_op jit(solution)/shard_map/all_gather | solution.py:77
  296.2 3.6 fusion.6
  300.7 23.3 %all-gather.10 = bf16[1,4,768]{1,0,2:T(2,128)(2,1)S(1)} all-gather(bf16[1,4,48]{1,0,2:T(2,128)(2,1)S(1)} %copy.292), channel_id=12, replica_groups=mesh['shard'=16,'context'=4,'tensor'=2] {'shard'}, dimensions={2}, use_global_device_ids=true | all-gather | bytes 6528 | tf_op jit(solution)/shard_map/all_gather | solution.py:79
  324.5 22.4 %all-gather.9 = bf16[1,2,768]{1,0,2:T(2,128)(2,1)S(1)} all-gather(bf16[1,2,48]{1,0,2:T(2,128)(2,1)S(1)} %copy.291), channel_id=11, replica_groups=mesh['shard'=16,'context'=4,'tensor'=2] {'shard'}, dimensions={2}, use_global_device_ids=true | all-gather | bytes 3264 | tf_op jit(solution)/shard_map/all_gather | solution.py:78
  347.3 22.1 %all-gather.12 = bf16[1,2,6,64]{2,1,0,3:T(2,128)(2,1)S(1)} all-gather(bf16[1,2,6,4]{2,1,0,3:T(2,128)(2,1)S(1)} %copy.293), channel_id=14, replica_groups=mesh['shard'=16,'context'=4,'tensor'=2] {'shard'}, dimensions={3}, use_global_device_ids=true | all-gather | bytes 1632 | tf_op jit(solution)/shard_map/all_gather | solution.py:73
  370.8 24.5 %all-gather.14 = bf16[1,384,768]{1,2,0:T(8,128)(2,1)} all-gather(bf16[1,384,48]{1,2,0:T(8,128)(2,1)S(1)} %get-tuple-element.104), channel_id=16, replica_groups=mesh['shard'=16,'context'=4,'tensor'=2] {'shard'}, dimensions={2}, use_global_device_ids=true | all-gather | bytes 626688 | tf_op jit(solution)/shard_map/all_gather | solution.py:74
  395.4 4.6 slice_reduce_fusion.2
  400.0 11.2 slice_reduce_fusion
  416.2 15.3 all-gather.13
  438.4 14.1 all_gather.89
  454.7 3.1 convolution_convert_fusion.4
  460.8 22.6 %all-gather.16 = bf16[1,24,64]{1,0,2:T(2,128)(2,1)S(1)} all-gather(bf16[1,24,4]{1,0,2:T(2,128)(2,1)S(1)} %copy.294), channel_id=18, replica_groups=mesh['shard'=16,'context'=4,'tensor'=2] {'shard'}, dimensions={2}, use_global_device_ids=true | all-gather | bytes 3264 | tf_op jit(solution)/shard_map/all_gather | solution.py:76
  486.8 44.9 %all-gather.33.cloned.1.call-done = bf16[1,768,1536]{2,1,0:T(8,128)(2,1)} async-done(((bf16[1,48,1536]{2,1,0:T(8,128)(2,1)}), bf16[1,768,1536]{2,1,0:T(8,128)(2,1)}) %all-gather.33.cloned.1.call-update) | async-done | bytes 2359312 | tf_op jit(solution)/shard_map/all_gather | solution.py:75
  531.7 3.7 convolution_add_fusion
  535.4 43.8 %all-gather.35.cloned.1.call-done = bf16[1,1536,768]{1,2,0:T(8,128)(2,1)} async-done(((bf16[1,1536,48]{1,2,0:T(8,128)(2,1)}), bf16[1,1536,768]{1,2,0:T(8,128)(2,1)}) %all-gather.35.cloned.1.call-update) | async-done | bytes 2359312 | tf_op jit(solution)/shard_map/all_gather | solution.py:77
  579.1 4.5 fusion.157
  586.1 4.1 fusion.3
  590.5 19.0 %all-reduce.36.cloned.1.call-done = bf16[2,128,768]{2,1,0:T(8,128)(2,1)} async-done(((bf16[2,128,768]{2,1,0:T(8,128)(2,1)}), bf16[2,128,768]{2,1,0:T(8,128)(2,1)}) %all-reduce.36.cloned.1.call-update) | async-done | bytes 393232 | tf_op jit(solution)/shard_map/psum | solution.py:216
  612.0 26.7 %all-reduce.34.cloned.1.call-done = f32[2,128,768]{2,1,0:T(8,128)} async-done(((f32[2,128,768]{2,1,0:T(8,128)}), f32[2,128,768]{2,1,0:T(8,128)}) %all-reduce.34.cloned.1.call-update) | async-done | bytes 786448 | tf_op jit(solution)/shard_map/psum | solution.py:138
  638.7 3.4 fusion.140
  646.9 3.5 multiply_convert_fusion.1
  652.8 2.4 copy.234
  655.3 3.8 convolution_convert_fusion.2
  661.5 2.4 fusion.146
  664.7 14.6 reduce-scatter.21.cloned.1.call-done
  679.2 24.7 %reduce-scatter.23.cloned.1.call-done = bf16[2,128,384]{2,1,0:T(8,128)(2,1)} async-done(((bf16[2,512,384]{2,1,0:T(8,128)(2,1)}), bf16[2,128,384]{2,1,0:T(8,128)(2,1)}) %reduce-scatter.23.cloned.1.call-update) | async-done | bytes 196624 | tf_op jit(solution)/shard_map/reduce_scatter | solution.py:255
  704.0 3.3 fusion.50
  707.3 24.0 %all-reduce.38.cloned.1.call-done = bf16[2,128,768]{2,1,0:T(8,128)(2,1)} async-done(((bf16[2,128,768]{2,1,0:T(8,128)(2,1)}), bf16[2,128,768]{2,1,0:T(8,128)(2,1)}) %all-reduce.38.cloned.1.call-update) | async-done | bytes 393232 | tf_op jit(solution)/shard_map/psum | solution.py:269
  738.9 25.5 %all-reduce.40.cloned.1.call-done = bf16[2,128,768]{2,1,0:T(8,128)(2,1)} async-done(((bf16[2,128,768]{2,1,0:T(8,128)(2,1)}), bf16[2,128,768]{2,1,0:T(8,128)(2,1)}) %all-reduce.40.cloned.1.call-update) | async-done | bytes 393232 | tf_op jit(solution)/shard_map/psum | solution.py:216
  772.2 3.5 multiply_convert_fusion
  780.8 3.9 convolution_convert_fusion
  787.0 3.0 fusion.145
  791.8 12.8 reduce-scatter.25.cloned.1.call-done
  804.6 24.5 %reduce-scatter.27.cloned.1.call-done = bf16[2,128,384]{2,1,0:T(8,128)(2,1)} async-done(((bf16[2,512,384]{2,1,0:T(8,128)(2,1)}), bf16[2,128,384]{2,1,0:T(8,128)(2,1)}) %reduce-scatter.27.cloned.1.call-update) | async-done | bytes 196624 | tf_op jit(solution)/shard_map/reduce_scatter | solution.py:255
  829.1 3.2 fusion.53
  832.4 2.5 fusion.43
  837.4 3.1 fusion.35
  840.5 5.3 copy.244
  847.9 5.2 copy.242
  857.7 3.9 bitcast_convert_fusion
  862.7 2.4 bitcast_convert_fusion.3
  866.7 2.4 bitcast_convert_fusion.1
  875.5 75.6 %all-reduce.12 = (bf16[2,6,64]{1,0,2:T(2,128)(2,1)S(1)}, bf16[2,6,64]{1,0,2:T(2,128)(2,1)S(1)}, bf16[24,64]{1,0:T(8,128)(2,1)S(1)}, bf16[24,64]{1,0:T(8,128)(2,1...) all-reduce(bf16[2,6,64]{1,0,2:T(2,128)(2,1)S(1)} %copy.249, ...), channel_id=27, replica_groups=mesh['shard'=16,'context'=4,'tensor'=2] {'shard'}, use_global_device_ids=true, to_apply=%region_44.45.clone | all-reduce | flops 13824 | bytes 55296
  956.3 52.0 %reduce-scatter.37.cloned.1.call-done = bf16[384,48]{0,1:T(8,128)(2,1)} async-done(((bf16[384,768]{0,1:T(8,128)(2,1)}), bf16[384,48]{0,1:T(8,128)(2,1)}) %reduce-scatter.37.cloned.1.call-update) | async-done | bytes 36880
  1008.4 111.1 %all-reduce.44.cloned.1.call-done = (bf16[3,768,384]{2,0,1:T(4,128)(2,1)}, bf16[3,768,384]{2,0,1:T(4,128)(2,1)}) async-done(((bf16[3,768,384]{2,0,1:T(4,128)(2,1)}, bf16[3,768,384]{2,0,1:T(4,128)(2,1)}), (bf16[3,768,384]{2,0,1:T(4,128)(2,1)}, bf16[3,768,384]{2,0,1:T(4,128)(2,1)})) %all-reduce.44.cloned.1.call-update) | async-done | bytes 3538960
  1122.7 75.1 %reduce-scatter.31.cloned.1.call-done = bf16[48,1536]{1,0:T(8,128)(2,1)} async-done(((bf16[768,1536]{1,0:T(8,128)(2,1)}), bf16[48,1536]{1,0:T(8,128)(2,1)}) %reduce-scatter.31.cloned.1.call-update) | async-done | bytes 147472 | tf_op jit(solution)/shard_map/reduce_scatter | solution.py:305
  1197.8 77.9 %reduce-scatter.35.cloned.1.call-done = bf16[1536,48]{0,1:T(8,128)(2,1)} async-done(((bf16[1536,768]{0,1:T(8,128)(2,1)}), bf16[1536,48]{0,1:T(8,128)(2,1)}) %reduce-scatter.35.cloned.1.call-update) | async-done | bytes 147472 | tf_op jit(solution)/shard_map/reduce_scatter | solution.py:317
  1275.7 77.7 %reduce-scatter.29.cloned.1.call-done = bf16[48,1536]{1,0:T(8,128)(2,1)} async-done(((bf16[768,1536]{1,0:T(8,128)(2,1)}), bf16[48,1536]{1,0:T(8,128)(2,1)}) %reduce-scatter.29.cloned.1.call-update) | async-done | bytes 147472 | tf_op jit(solution)/shard_map/reduce_scatter | solution.py:305
  1353.3 77.9 %reduce-scatter.33.cloned.1.call-done = bf16[1536,48]{0,1:T(8,128)(2,1)} async-done(((bf16[1536,768]{0,1:T(8,128)(2,1)}), bf16[1536,48]{0,1:T(8,128)(2,1)}) %reduce-scatter.33.cloned.1.call-update) | async-done | bytes 147472 | tf_op jit(solution)/shard_map/reduce_scatter | solution.py:317
  1432.5 43.3 %all-reduce.46.cloned.1.call-done = (bf16[1,2,6,4]{2,3,1,0:T(4,128)(2,1)}, bf16[1,2,6,4]{2,3,1,0:T(4,128)(2,1)}, bf16[1,384,48]{1,2,0:T(8,128)(2,1)}, bf16[1,384...) async-done(((bf16[1,2,6,4]{2,3,1,0:T(4,128)(2,1)}, ...) | async-done | bytes 75472 | tf_op jit(solution)/shard_map/psum | solution.py:292
  1482.4 42.9 %all-reduce.48.cloned.1.call-done = (bf16[1,3,48,384]{3,1,2,0:T(4,128)(2,1)}, bf16[1,3,48,384]{3,1,2,0:T(4,128)(2,1)}, bf16[1,48,1536]{2,1,0:T(8,128)(2,1)}, bf1...) async-done(((bf16[1,3,48,384]{3,1,2,0:T(4,128)(2,1)}, bf16[1,3,48,384]{3,1,2,0:T(4,128)(2,1)}, bf16[1,48,1536]{2,1,0:T(8,128)(2,1)}, ...) | async-done | bytes 811024 | tf_op jit(solution)/shard_map/psum | solution.py:286
  (409 shorter events, 124.9 us)
Async XLA Ops:
  7.2 29.1 %copy-start.83 = (bf16[2,2,48]{2,1,0:T(2,128)(2,1)S(1)}, bf16[2,2,48]{2,1,0:T(2,128)(2,1)}, u32[]{:S(2)}) copy-start(bf16[2,2,48]{2,1,0:T(2,128)(2,1)} %param.19) | copy-start | bytes 1156
  7.2 53.6 %copy-start.88 = (s32[2,128]{1,0:T(2,128)S(1)}, s32[2,128]{1,0:T(2,128)}, u32[]{:S(2)}) copy-start(s32[2,128]{1,0:T(2,128)} %param.12) | copy-start | bytes 3076
  7.2 53.6 %copy-start.76 = (bf16[2,2,6,4]{2,3,1,0:T(4,128)(2,1)S(1)}, bf16[2,2,6,4]{2,3,1,0:T(4,128)(2,1)}, u32[]{:S(2)}) copy-start(bf16[2,2,6,4]{2,3,1,0:T(4,128)(2,1)} %param.14) | copy-start | bytes 580
  7.2 75.7 %copy-start = (f32[2,128,768]{2,1,0:T(8,128)S(1)}, f32[2,128,768]{2,1,0:T(8,128)}, u32[]{:S(2)}) copy-start(f32[2,128,768]{2,1,0:T(8,128)} %param.11) | copy-start | bytes 2359300
  7.2 126.0 %all-gather.25.cloned.1.call-start = ((), (), s32[]{:S(2)}) async-start(), calls=%async_computation.26 | async-start | bytes 1880064 | tf_op jit(solution)/shard_map/all_gather | solution.py:72
  9.0 84.1 %copy-start.41 = (bf16[2,384,48]{1,2,0:T(8,128)(2,1)S(1)}, bf16[2,384,48]{1,2,0:T(8,128)(2,1)}, u32[]{:S(2)}) copy-start(bf16[2,384,48]{1,2,0:T(8,128)(2,1)} %param.15) | copy-start | bytes 221188
  9.0 190.7 %all-reduce.28.cloned.1.call-start = ((), (), s32[]{:S(2)}) async-start(), calls=%async_computation.10 | async-start | bytes 1572864 | tf_op jit(solution)/shard_map/psum | solution.py:128
  82.8 71.6 %copy-start.50 = (f32[6,64]{1,0:T(8,128)}, f32[6,64]{1,0:T(8,128)S(1)}, u32[]{:S(2)}) copy-start(f32[6,64]{1,0:T(8,128)S(1)} %copy.213) | copy-start | bytes 4612
  117.0 57.7 %copy-start.10 = (bf16[1,384,768]{1,2,0:T(8,128)(2,1)}, bf16[1,384,768]{1,2,0:T(8,128)(2,1)S(1)}, u32[]{:S(2)}) copy-start(bf16[1,384,768]{1,2,0:T(8,128)(2,1)S(1)} %all-gather.5) | copy-start | bytes 1769476
  117.0 18.5 %copy-start.46 = (f32[2,128]{1,0:T(2,128)}, f32[2,128]{1,0:T(2,128)S(1)}, u32[]{:S(2)}) copy-start(f32[2,128]{1,0:T(2,128)S(1)} %broadcast_multiply_fusion.11) | copy-start | bytes 3076
  121.8 13.7 copy-start.53
  122.1 49.4 %copy-start.20 = (pred[2,128,512]{2,1,0:T(8,128)(4,1)}, pred[2,128,512]{2,1,0:T(8,128)(4,1)S(1)}, u32[]{:S(2)}) copy-start(pred[2,128,512]{2,1,0:T(8,128)(4,1)S(1)} %compare_and_fusion) | copy-start | bytes 393220
  133.2 115.2 %copy-start.61 = (f32[768]{0:T(1024)}, f32[768]{0:T(1024)S(1)}, u32[]{:S(2)}) copy-start(f32[768]{0:T(1024)S(1)} %get-tuple-element.49) | copy-start | bytes 9220
  157.9 13.7 copy-start.71
  176.1 72.3 %all-gather.27.cloned.1.call-start = ((), (), s32[]{:S(2)}) async-start(), calls=%async_computation.27 | async-start | bytes 2506752 | tf_op jit(solution)/shard_map/all_gather | solution.py:75
  176.9 119.4 %all-gather.29.cloned.1.call-start = ((), (), s32[]{:S(2)}) async-start(), calls=%async_computation.28 | async-start | bytes 2506752 | tf_op jit(solution)/shard_map/all_gather | solution.py:77
  177.7 233.5 %all-reduce.30.cloned.1.call-start = ((), (), s32[]{:S(2)}) async-start(), calls=%async_computation.11 | async-start | bytes 1572864 | tf_op jit(solution)/shard_map/psum | solution.py:138
  201.1 49.8 %copy-start.55 = (f32[2,128]{1,0:T(2,128)}, f32[2,128]{1,0:T(2,128)S(1)}, u32[]{:S(2)}) copy-start(f32[2,128]{1,0:T(2,128)S(1)} %broadcast_multiply_fusion.10) | copy-start | bytes 3076
  201.3 49.6 %copy-start.64 = (f32[2,128]{1,0:T(2,128)}, f32[2,128]{1,0:T(2,128)S(1)}, u32[]{:S(2)}) copy-start(f32[2,128]{1,0:T(2,128)S(1)} %add_rsqrt_fusion.2) | copy-start | bytes 3076
  250.9 45.3 %copy-start.90 = (f32[2,128,1536]{2,1,0:T(8,128)}, f32[2,128,1536]{2,1,0:T(8,128)S(1)}, u32[]{:S(2)}) copy-start(f32[2,128,1536]{2,1,0:T(8,128)S(1)} %convolution_add_fusion.1) | copy-start | bytes 4718596
  250.9 49.6 %copy-start.79 = (bf16[1,4,48]{2,1,0:T(4,128)(2,1)S(1)}, bf16[1,4,48]{2,1,0:T(4,128)(2,1)}, u32[]{:S(2)}) copy-start(bf16[1,4,48]{2,1,0:T(4,128)(2,1)} %get-tuple-element.115) | copy-start | bytes 1156
  299.9 24.5 %copy-start.82 = (bf16[1,2,48]{2,1,0:T(2,128)(2,1)S(1)}, bf16[1,2,48]{2,1,0:T(2,128)(2,1)}, u32[]{:S(2)}) copy-start(bf16[1,2,48]{2,1,0:T(2,128)(2,1)} %get-tuple-element.116) | copy-start | bytes 580
  299.9 47.4 %copy-start.75 = (bf16[1,2,6,4]{2,3,1,0:T(4,128)(2,1)S(1)}, bf16[1,2,6,4]{2,3,1,0:T(4,128)(2,1)}, u32[]{:S(2)}) copy-start(bf16[1,2,6,4]{2,3,1,0:T(4,128)(2,1)} %get-tuple-element.110) | copy-start | bytes 292
  299.9 112.8 %all-gather.31.cloned.1.call-start = ((), (), s32[]{:S(2)}) async-start(), calls=%async_computation.29 | async-start | bytes 1880064 | tf_op jit(solution)/shard_map/all_gather | solution.py:72
  300.5 183.7 %all-reduce.32.cloned.1.call-start = ((), (), s32[]{:S(2)}) async-start(), calls=%async_computation.12 | async-start | bytes 1572864 | tf_op jit(solution)/shard_map/psum | solution.py:128
  437.2 17.6 %copy-start.22 = (pred[2,128,512]{2,1,0:T(8,128)(4,1)S(1)}, pred[2,128,512]{2,1,0:T(8,128)(4,1)}, u32[]{:S(2)}) copy-start(pred[2,128,512]{2,1,0:T(8,128)(4,1)} %copy-done.20) | copy-start | bytes 393220
  437.2 20.7 %copy-start.73 = (f32[2,6,128]{2,1,0:T(8,128)}, f32[2,6,128]{2,1,0:T(8,128)S(1)}, u32[]{:S(2)}) copy-start(f32[2,6,128]{2,1,0:T(8,128)S(1)} %log_add_fusion) | copy-start | bytes 18436
  457.9 26.3 %copy-start.28 = (bf16[2,6,64,128]{3,2,1,0:T(8,128)(2,1)}, bf16[2,6,64,128]{3,2,1,0:T(8,128)(2,1)S(1)}, u32[]{:S(2)}) copy-start(bf16[2,6,64,128]{3,2,1,0:T(8,128)(2,1)S(1)} %convolution_convert_fusion.4) | copy-start | bytes 589828
  459.3 72.4 %all-gather.33.cloned.1.call-start = ((), (), s32[]{:S(2)}) async-start(), calls=%async_computation.30 | async-start | bytes 2506752 | tf_op jit(solution)/shard_map/all_gather | solution.py:75
  460.0 119.1 %all-gather.35.cloned.1.call-start = ((), (), s32[]{:S(2)}) async-start(), calls=%async_computation.31 | async-start | bytes 2506752 | tf_op jit(solution)/shard_map/all_gather | solution.py:77
  460.7 148.8 %all-reduce.36.cloned.1.call-start = ((), (), s32[]{:S(2)}) async-start(), calls=%async_computation.14 | async-start | bytes 786432 | tf_op jit(solution)/shard_map/psum | solution.py:216
  579.1 5.3 copy-start.86
  586.1 52.6 %all-reduce.34.cloned.1.call-start = ((), (), s32[]{:S(2)}) async-start(), calls=%async_computation.13 | async-start | bytes 1572864 | tf_op jit(solution)/shard_map/psum | solution.py:138
  590.2 89.0 %reduce-scatter.21.cloned.1.call-start = ((), (), s32[]{:S(2)}) async-start(), calls=%async_computation.15 | async-start | bytes 983040 | tf_op jit(solution)/shard_map/reduce_scatter | solution.py:252
  655.2 48.7 %reduce-scatter.23.cloned.1.call-start = ((), (), s32[]{:S(2)}) async-start(), calls=%async_computation.16 | async-start | bytes 983040 | tf_op jit(solution)/shard_map/reduce_scatter | solution.py:255
  661.4 69.9 %all-reduce.38.cloned.1.call-start = ((), (), s32[]{:S(2)}) async-start(), calls=%async_computation.17 | async-start | bytes 786432 | tf_op jit(solution)/shard_map/psum | solution.py:269
  704.0 27.3 %copy-start.49 = (f32[2,128]{1,0:T(2,128)S(1)}, f32[2,128]{1,0:T(2,128)}, u32[]{:S(2)}) copy-start(f32[2,128]{1,0:T(2,128)} %copy-done.48) | copy-start | bytes 3076
  704.0 27.3 %copy-start.58 = (f32[2,128]{1,0:T(2,128)S(1)}, f32[2,128]{1,0:T(2,128)}, u32[]{:S(2)}) copy-start(f32[2,128]{1,0:T(2,128)} %copy-done.57) | copy-start | bytes 3076
  707.2 57.2 %all-reduce.40.cloned.1.call-start = ((), (), s32[]{:S(2)}) async-start(), calls=%async_computation.18 | async-start | bytes 786432 | tf_op jit(solution)/shard_map/psum | solution.py:216
  737.3 27.1 %copy-start.56 = (f32[2,128]{1,0:T(2,128)S(1)}, f32[2,128]{1,0:T(2,128)}, u32[]{:S(2)}) copy-start(f32[2,128]{1,0:T(2,128)} %copy-done.55) | copy-start | bytes 3076
  737.3 27.1 %copy-start.65 = (f32[2,128]{1,0:T(2,128)S(1)}, f32[2,128]{1,0:T(2,128)}, u32[]{:S(2)}) copy-start(f32[2,128]{1,0:T(2,128)} %copy-done.64) | copy-start | bytes 3076
  738.9 65.7 %reduce-scatter.25.cloned.1.call-start = ((), (), s32[]{:S(2)}) async-start(), calls=%async_computation.19 | async-start | bytes 983040 | tf_op jit(solution)/shard_map/reduce_scatter | solution.py:252
  765.9 5.3 copy-start.27
  772.2 4.7 copy-start.18
  772.2 4.7 copy-start.51
  780.5 48.5 %reduce-scatter.27.cloned.1.call-start = ((), (), s32[]{:S(2)}) async-start(), calls=%async_computation.20 | async-start | bytes 983040 | tf_op jit(solution)/shard_map/reduce_scatter | solution.py:255
  787.0 85.9 %all-reduce.42.cloned.1.call-start = ((), (), s32[]{:S(2)}) async-start(), calls=%async_computation.21 | async-start | bytes 786432 | tf_op jit(solution)/shard_map/psum | solution.py:269
  832.3 123.9 %reduce-scatter.39.cloned.1.call-start = ((), (), s32[]{:S(2)}) async-start(), calls=%async_computation.33 | async-start | bytes 626688
  834.9 173.4 %reduce-scatter.37.cloned.1.call-start = ((), (), s32[]{:S(2)}) async-start(), calls=%async_computation.32 | async-start | bytes 626688
  837.3 282.1 %all-reduce.44.cloned.1.call-start = ((), (), s32[]{:S(2)}) async-start(), calls=%async_computation.34 | async-start | bytes 9437184
  840.5 5.3 copy-start.39
  840.5 5.3 copy-start.40
  840.5 5.3 copy-start.43
  840.5 5.3 copy-start.47
  840.5 5.3 copy-start.54
  840.5 5.3 copy-start.87
  853.1 344.7 %reduce-scatter.31.cloned.1.call-start = ((), (), s32[]{:S(2)}) async-start(), calls=%async_computation.23 | async-start | bytes 2506752 | tf_op jit(solution)/shard_map/reduce_scatter | solution.py:305
  856.6 419.0 %reduce-scatter.35.cloned.1.call-start = ((), (), s32[]{:S(2)}) async-start(), calls=%async_computation.25 | async-start | bytes 2506752 | tf_op jit(solution)/shard_map/reduce_scatter | solution.py:317
  861.6 491.7 %reduce-scatter.29.cloned.1.call-start = ((), (), s32[]{:S(2)}) async-start(), calls=%async_computation.22 | async-start | bytes 2506752 | tf_op jit(solution)/shard_map/reduce_scatter | solution.py:305
  865.1 566.1 %reduce-scatter.33.cloned.1.call-start = ((), (), s32[]{:S(2)}) async-start(), calls=%async_computation.24 | async-start | bytes 2506752 | tf_op jit(solution)/shard_map/reduce_scatter | solution.py:317
  869.2 606.6 %all-reduce.46.cloned.1.call-start = ((), (), s32[]{:S(2)}) async-start(), calls=%async_computation.35 | async-start | bytes 165888 | tf_op jit(solution)/shard_map/psum | solution.py:292
  872.7 558.6 %copy-start.4 = (f32[2,128,768]{2,1,0:T(8,128)S(1)}, f32[2,128,768]{2,1,0:T(8,128)}, u32[]{:S(2)}) copy-start(f32[2,128,768]{2,1,0:T(8,128)} %copy-done.3) | copy-start | bytes 2359300
  872.9 558.4 %copy-start.19 = (bf16[2,128,768]{2,1,0:T(8,128)(2,1)S(1)}, bf16[2,128,768]{2,1,0:T(8,128)(2,1)}, u32[]{:S(2)}) copy-start(bf16[2,128,768]{2,1,0:T(8,128)(2,1)} %all-reduce.42.cloned.1.call-done) | copy-start | bytes 1179652
  1008.3 516.9 %all-reduce.48.cloned.1.call-start = ((), (), s32[]{:S(2)}) async-start(), calls=%async_computation.36 | async-start | bytes 1769472 | tf_op jit(solution)/shard_map/psum | solution.py:286
  (56 other events, 127.4 us)
Sparse Core Ops, SparseCore 0:
  10.8 47.1 all-gather.24
  176.2 21.9 all-reduce.27
  201.2 47.1 all-gather.26
  251.2 45.0 all-gather.28
  300.0 24.0 all-reduce.29
  326.1 46.5 all-gather.30
  459.4 22.1 all-reduce.31
  484.5 47.1 all-gather.32
  534.0 45.0 all-gather.34
  586.2 23.2 all-reduce.35
  612.5 26.1 all-reduce.33
  655.4 23.8 reduce-scatter.20
  681.8 22.1 reduce-scatter.22
  707.4 23.8 all-reduce.37
  739.0 25.3 all-reduce.39
  780.6 23.8 reduce-scatter.24
  806.9 22.0 reduce-scatter.26
  832.5 23.8 all-reduce.41
  860.1 73.2 reduce-scatter.38
  937.1 71.1 reduce-scatter.36
  1011.7 107.6 all-reduce.43
  1123.1 74.6 reduce-scatter.30
  1201.4 74.1 reduce-scatter.34
  1279.2 74.1 reduce-scatter.28
  1357.0 74.2 reduce-scatter.32
  1435.6 40.1 all-reduce.45
  1479.0 46.2 all-reduce.47
where the time goes:
time: 1540 us
  waiting for transfers between devices  913 us (59%)
  blocking collectives  373 us (24%)
  local copies, waits for them, and re-layouts  101 us (7%)
  matrix products  92.7 us (6%)
  other arithmetic  40.6 us (3%)
  between operations  17.3 us (1%)
    unnamed x30, waiting for transfers between devices  165 us
    reduce_scatter x2, waiting for transfers between devices, per_device(): lax.psum_scatter(grad_parts[5].astype(jnp.bfloat16), 'shard', scatter_dim...  156 us
    reduce_scatter x2, waiting for transfers between devices, per_device(): lax.psum_scatter(grad_parts[3].astype(jnp.bfloat16), 'shard', scatter_dim...  153 us
    all_gather x2, waiting for transfers between devices, per_device(): lax.all_gather(expansion[layer_index], 'shard', axis=0, tiled=True)  91.9 us
    all_gather x2, waiting for transfers between devices, per_device(): lax.all_gather(contraction[layer_index], 'shard', axis=1, tiled=True)  89.1 us
    unnamed x1, blocking collectives  75.6 us
    reduce_scatter x2, waiting for transfers between devices, per_device(): lax.psum_scatter(value_full.astype(jnp.bfloat16), 'context', scatter_dime...  49.3 us
    all_gather x2, blocking collectives, per_device(): lax.all_gather(offsets[layer_index], 'shard', axis=1, tiled=True)  48.7 us
  transfers between devices with their start and end apart: 27, of which 20 were waited for; matrix products, arithmetic and copies ran while one was open for 9% of the time, Pallas kernels for 0%

commit v1 on v0

--- a/solution.py
+++ b/solution.py
@@ -8,6 +8,11 @@
 GELU_COEF = 0.7978845608028654
 GELU_CUBE = 0.044715
 MASKED = -1e30
+
+
+def summed_here(x, mesh_axis):
+    shards = lax.all_gather(x, mesh_axis)
+    return jnp.sum(shards, axis=0)
 
 
 def gelu_value(preact):
@@ -213,7 +218,7 @@
         feed_partial = jnp.einsum(
             "rtf,df->rtd", hidden_half, up_weight, preferred_element_type=jnp.float32
         )
-        feed_back = lax.psum(feed_partial.astype(jnp.bfloat16), "tensor").astype(jnp.float32)
+        feed_back = summed_here(feed_partial.astype(jnp.bfloat16), "tensor").astype(jnp.float32)
         gain_two = jnp.sum(feed_back * normed_two, axis=(0, 1))
         offset_two = jnp.sum(feed_back, axis=(0, 1))
         middle_back = upstream + norm_backward(feed_back, normed_two, spread_two, gain_float[1])

time: 1540 us -> 1490 us (0.968)
  waiting for transfers between devices: 913 us -> 856 us
    psum x2 -> x0, waiting for transfers between devices: 44.5 us -> none  [per_device(): lax.psum(feed_partial.astype(jnp.bfloat16), 'tensor').astype(jnp.float32)]
    unnamed x30 -> x28, waiting for transfers between devices: 165 us -> 165 us
  transfers between devices with their start and end apart: 27 -> 25, of which waited for: 20 -> 18; matrix products, arithmetic and copies ran while one was open for 9% -> 9% of each run, Pallas kernels for 0% -> 0%
where the time goes in v1:
time: 1490 us; the launch traced here: 1480 us
  waiting for transfers between devices  856 us (57%)
  blocking collectives  377 us (25%)
  local copies, waits for them, and re-layouts  96.9 us (7%)
  matrix products  91.8 us (6%)
  other arithmetic  44 us (3%)
  between operations  17.1 us (1%)
    unnamed x28, waiting for transfers between devices  165 us
    reduce_scatter x2, waiting for transfers between devices, per_device(): lax.psum_scatter(grad_parts[5].astype(jnp.bfloat16), 'shard', scatter_dim...  156 us
    reduce_scatter x2, waiting for transfers between devices, per_device(): lax.psum_scatter(grad_parts[3].astype(jnp.bfloat16), 'shard', scatter_dim...  153 us
    all_gather x2, waiting for transfers between devices, per_device(): lax.all_gather(expansion[layer_index], 'shard', axis=0, tiled=True)  93.6 us
    all_gather x2, waiting for transfers between devices, per_device(): lax.all_gather(contraction[layer_index], 'shard', axis=1, tiled=True)  89.1 us
    unnamed x1, blocking collectives  75.5 us
    reduce_scatter x2, waiting for transfers between devices, per_device(): lax.psum_scatter(value_full.astype(jnp.bfloat16), 'context', scatter_dime...  49.1 us
    all_gather x2, blocking collectives, per_device(): lax.all_gather(offsets[layer_index], 'shard', axis=1, tiled=True)  48.7 us
  transfers between devices with their start and end apart: 25, of which 18 were waited for; matrix products, arithmetic and copies ran while one was open for 9% of the time, Pallas kernels for 0%

profile of v1, /device:TPU:0, one launch (start us, length us, event | category | flops | bytes accessed | tf_op | source)
XLA Modules:
  0.0 1483.9 jit_solution(17113137418452583356)
XLA Ops:
  10.4 25.5 %all-gather.1 = bf16[1,4,768]{1,0,2:T(2,128)(2,1)S(1)} all-gather(bf16[1,4,48]{1,0,2:T(2,128)(2,1)S(1)} %copy.288), channel_id=3, replica_groups=mesh['shard'=16,'context'=4,'tensor'=2] {'shard'}, dimensions={2}, use_global_device_ids=true | all-gather | bytes 6528 | tf_op jit(solution)/shard_map/all_gather | solution.py:84
  37.0 23.4 %all-gather = bf16[1,2,768]{1,0,2:T(2,128)(2,1)S(1)} all-gather(bf16[1,2,48]{1,0,2:T(2,128)(2,1)S(1)} %copy.287), channel_id=2, replica_groups=mesh['shard'=16,'context'=4,'tensor'=2] {'shard'}, dimensions={2}, use_global_device_ids=true | all-gather | bytes 3264 | tf_op jit(solution)/shard_map/all_gather | solution.py:83
  61.4 21.3 %all-gather.3 = bf16[1,2,6,64]{2,1,0,3:T(2,128)(2,1)S(1)} all-gather(bf16[1,2,6,4]{2,1,0,3:T(2,128)(2,1)S(1)} %copy.289), channel_id=5, replica_groups=mesh['shard'=16,'context'=4,'tensor'=2] {'shard'}, dimensions={3}, use_global_device_ids=true | all-gather | bytes 1632 | tf_op jit(solution)/shard_map/all_gather | solution.py:78
  83.1 10.0 all_gather.91
  93.1 23.9 %all-gather.5 = bf16[1,384,768]{1,2,0:T(8,128)(2,1)S(1)} all-gather(bf16[1,384,48]{1,2,0:T(8,128)(2,1)S(1)} %get-tuple-element.105), channel_id=7, replica_groups=mesh['shard'=16,'context'=4,'tensor'=2] {'shard'}, dimensions={2}, use_global_device_ids=true | all-gather | bytes 626688 | tf_op jit(solution)/shard_map/all_gather | solution.py:79
  117.2 4.6 slice_reduce_fusion.8
  122.1 11.0 slice_reduce_fusion.6
  136.3 14.4 all-gather.4
  157.9 13.3 all_gather.90
  171.6 3.1 convolution_convert_fusion.5
  178.3 21.3 %all-gather.7 = bf16[1,24,64]{1,0,2:T(2,128)(2,1)S(1)} all-gather(bf16[1,24,4]{1,0,2:T(2,128)(2,1)S(1)} %copy.290), channel_id=9, replica_groups=mesh['shard'=16,'context'=4,'tensor'=2] {'shard'}, dimensions={2}, use_global_device_ids=true | all-gather | bytes 3264 | tf_op jit(solution)/shard_map/all_gather | solution.py:81
  201.3 47.0 %all-gather.29.cloned.1.call-done = bf16[1,768,1536]{2,1,0:T(8,128)(2,1)} async-done(((bf16[1,48,1536]{2,1,0:T(8,128)(2,1)}), bf16[1,768,1536]{2,1,0:T(8,128)(2,1)}) %all-gather.29.cloned.1.call-update) | async-done | bytes 2359312 | tf_op jit(solution)/shard_map/all_gather | solution.py:80
  248.4 2.5 convolution_add_fusion.1
  250.9 45.3 %all-gather.31.cloned.1.call-done = bf16[1,1536,768]{1,2,0:T(8,128)(2,1)} async-done(((bf16[1,1536,48]{1,2,0:T(8,128)(2,1)}), bf16[1,1536,768]{1,2,0:T(8,128)(2,1)}) %all-gather.31.cloned.1.call-update) | async-done | bytes 2359312 | tf_op jit(solution)/shard_map/all_gather | solution.py:82
  296.3 3.6 fusion.6
  300.7 23.3 %all-gather.10 = bf16[1,4,768]{1,0,2:T(2,128)(2,1)S(1)} all-gather(bf16[1,4,48]{1,0,2:T(2,128)(2,1)S(1)} %copy.292), channel_id=12, replica_groups=mesh['shard'=16,'context'=4,'tensor'=2] {'shard'}, dimensions={2}, use_global_device_ids=true | all-gather | bytes 6528 | tf_op jit(solution)/shard_map/all_gather | solution.py:84
  324.5 22.4 %all-gather.9 = bf16[1,2,768]{1,0,2:T(2,128)(2,1)S(1)} all-gather(bf16[1,2,48]{1,0,2:T(2,128)(2,1)S(1)} %copy.291), channel_id=11, replica_groups=mesh['shard'=16,'context'=4,'tensor'=2] {'shard'}, dimensions={2}, use_global_device_ids=true | all-gather | bytes 3264 | tf_op jit(solution)/shard_map/all_gather | solution.py:83
  347.3 22.1 %all-gather.12 = bf16[1,2,6,64]{2,1,0,3:T(2,128)(2,1)S(1)} all-gather(bf16[1,2,6,4]{2,1,0,3:T(2,128)(2,1)S(1)} %copy.293), channel_id=14, replica_groups=mesh['shard'=16,'context'=4,'tensor'=2] {'shard'}, dimensions={3}, use_global_device_ids=true | all-gather | bytes 1632 | tf_op jit(solution)/shard_map/all_gather | solution.py:78
  370.8 24.5 %all-gather.14 = bf16[1,384,768]{1,2,0:T(8,128)(2,1)} all-gather(bf16[1,384,48]{1,2,0:T(8,128)(2,1)S(1)} %get-tuple-element.104), channel_id=16, replica_groups=mesh['shard'=16,'context'=4,'tensor'=2] {'shard'}, dimensions={2}, use_global_device_ids=true | all-gather | bytes 626688 | tf_op jit(solution)/shard_map/all_gather | solution.py:79
  395.4 4.6 slice_reduce_fusion.2
  399.9 11.2 slice_reduce_fusion
  416.2 15.3 %all-gather.13 = bf16[1,2,512,384]{3,2,0,1:T(8,128)(2,1)} all-gather(bf16[1,2,128,384]{3,2,0,1:T(8,128)(2,1)S(1)} %slice.234), channel_id=15, replica_groups=mesh['shard'=16,'context'=4,'tensor'=2] {'context'}, dimensions={2}, use_global_device_ids=true | all-gather | bytes 983040 | tf_op jit(solution)/shard_map/all_gather | solution.py:108
  438.6 13.3 all_gather.101
  453.0 3.1 convolution_convert_fusion.4
  459.7 22.5 %all-gather.16 = bf16[1,24,64]{1,0,2:T(2,128)(2,1)S(1)} all-gather(bf16[1,24,4]{1,0,2:T(2,128)(2,1)S(1)} %copy.294), channel_id=18, replica_groups=mesh['shard'=16,'context'=4,'tensor'=2] {'shard'}, dimensions={2}, use_global_device_ids=true | all-gather | bytes 3264 | tf_op jit(solution)/shard_map/all_gather | solution.py:81
  484.0 46.6 %all-gather.35.cloned.1.call-done = bf16[1,768,1536]{2,1,0:T(8,128)(2,1)} async-done(((bf16[1,48,1536]{2,1,0:T(8,128)(2,1)}), bf16[1,768,1536]{2,1,0:T(8,128)(2,1)}) %all-gather.35.cloned.1.call-update) | async-done | bytes 2359312 | tf_op jit(solution)/shard_map/all_gather | solution.py:80
  530.6 3.7 convolution_add_fusion
  534.3 43.8 %all-gather.37.cloned.1.call-done = bf16[1,1536,768]{1,2,0:T(8,128)(2,1)} async-done(((bf16[1,1536,48]{1,2,0:T(8,128)(2,1)}), bf16[1,1536,768]{1,2,0:T(8,128)(2,1)}) %all-gather.37.cloned.1.call-update) | async-done | bytes 2359312 | tf_op jit(solution)/shard_map/all_gather | solution.py:82
  578.0 4.1 fusion.3
  582.2 4.5 fusion.157
  587.5 2.7 all-gather.18
  593.7 12.6 all-reduce.32.cloned.1.call-done
  606.3 3.3 fusion.140
  614.4 3.5 multiply_convert_fusion.1
  622.7 3.8 convolution_convert_fusion.2
  628.9 2.9 fusion.146
  632.0 14.6 reduce-scatter.21.cloned.1.call-done
  646.6 24.5 %reduce-scatter.23.cloned.1.call-done = bf16[2,128,384]{2,1,0:T(8,128)(2,1)} async-done(((bf16[2,512,384]{2,1,0:T(8,128)(2,1)}), bf16[2,128,384]{2,1,0:T(8,128)(2,1)}) %reduce-scatter.23.cloned.1.call-update) | async-done | bytes 196624 | tf_op jit(solution)/shard_map/reduce_scatter | solution.py:260
  671.1 3.2 fusion.50
  674.4 23.9 %all-reduce.34.cloned.1.call-done = bf16[2,128,768]{2,1,0:T(8,128)(2,1)} async-done(((bf16[2,128,768]{2,1,0:T(8,128)(2,1)}), bf16[2,128,768]{2,1,0:T(8,128)(2,1)}) %all-reduce.34.cloned.1.call-update) | async-done | bytes 393232 | tf_op jit(solution)/shard_map/psum | solution.py:274
  705.3 2.5 all-gather.19
  717.6 3.5 multiply_convert_fusion
  726.2 3.9 convolution_convert_fusion
  730.1 2.4 copy.239
  732.6 3.0 fusion.145
  737.4 12.6 reduce-scatter.25.cloned.1.call-done
  750.0 24.6 %reduce-scatter.27.cloned.1.call-done = bf16[2,128,384]{2,1,0:T(8,128)(2,1)} async-done(((bf16[2,512,384]{2,1,0:T(8,128)(2,1)}), bf16[2,128,384]{2,1,0:T(8,128)(2,1)}) %reduce-scatter.27.cloned.1.call-update) | async-done | bytes 196624 | tf_op jit(solution)/shard_map/reduce_scatter | solution.py:260
  774.6 3.3 fusion.53
  777.9 2.5 fusion.43
  782.9 3.1 fusion.35
  786.0 5.3 copy.244
  793.4 5.2 copy.242
  803.2 3.9 bitcast_convert_fusion
  808.2 2.4 bitcast_convert_fusion.3
  812.2 2.4 bitcast_convert_fusion.1
  821.2 75.5 %all-reduce.12 = (bf16[2,6,64]{1,0,2:T(2,128)(2,1)S(1)}, bf16[2,6,64]{1,0,2:T(2,128)(2,1)S(1)}, bf16[24,64]{1,0:T(8,128)(2,1)S(1)}, bf16[24,64]{1,0:T(8,128)(2,1...) all-reduce(bf16[2,6,64]{1,0,2:T(2,128)(2,1)S(1)} %copy.249, ...), channel_id=29, replica_groups=mesh['shard'=16,'context'=4,'tensor'=2] {'shard'}, use_global_device_ids=true, to_apply=%region_44.45.clone | all-reduce | flops 13824 | bytes 55296
  901.9 51.6 %reduce-scatter.37.cloned.1.call-done = bf16[384,48]{0,1:T(8,128)(2,1)} async-done(((bf16[384,768]{0,1:T(8,128)(2,1)}), bf16[384,48]{0,1:T(8,128)(2,1)}) %reduce-scatter.37.cloned.1.call-update) | async-done | bytes 36880
  953.6 111.1 %all-reduce.38.cloned.1.call-done = (bf16[3,768,384]{2,0,1:T(4,128)(2,1)}, bf16[3,768,384]{2,0,1:T(4,128)(2,1)}) async-done(((bf16[3,768,384]{2,0,1:T(4,128)(2,1)}, bf16[3,768,384]{2,0,1:T(4,128)(2,1)}), (bf16[3,768,384]{2,0,1:T(4,128)(2,1)}, bf16[3,768,384]{2,0,1:T(4,128)(2,1)})) %all-reduce.38.cloned.1.call-update) | async-done | bytes 3538960
  1067.9 75.0 %reduce-scatter.31.cloned.1.call-done = bf16[48,1536]{1,0:T(8,128)(2,1)} async-done(((bf16[768,1536]{1,0:T(8,128)(2,1)}), bf16[48,1536]{1,0:T(8,128)(2,1)}) %reduce-scatter.31.cloned.1.call-update) | async-done | bytes 147472 | tf_op jit(solution)/shard_map/reduce_scatter | solution.py:310
  1142.9 78.0 %reduce-scatter.35.cloned.1.call-done = bf16[1536,48]{0,1:T(8,128)(2,1)} async-done(((bf16[1536,768]{0,1:T(8,128)(2,1)}), bf16[1536,48]{0,1:T(8,128)(2,1)}) %reduce-scatter.35.cloned.1.call-update) | async-done | bytes 147472 | tf_op jit(solution)/shard_map/reduce_scatter | solution.py:322
  1220.9 77.9 %reduce-scatter.29.cloned.1.call-done = bf16[48,1536]{1,0:T(8,128)(2,1)} async-done(((bf16[768,1536]{1,0:T(8,128)(2,1)}), bf16[48,1536]{1,0:T(8,128)(2,1)}) %reduce-scatter.29.cloned.1.call-update) | async-done | bytes 147472 | tf_op jit(solution)/shard_map/reduce_scatter | solution.py:310
  1298.8 77.8 %reduce-scatter.33.cloned.1.call-done = bf16[1536,48]{0,1:T(8,128)(2,1)} async-done(((bf16[1536,768]{0,1:T(8,128)(2,1)}), bf16[1536,48]{0,1:T(8,128)(2,1)}) %reduce-scatter.33.cloned.1.call-update) | async-done | bytes 147472 | tf_op jit(solution)/shard_map/reduce_scatter | solution.py:322
  1377.8 43.4 %all-reduce.40.cloned.1.call-done = (bf16[1,2,6,4]{2,3,1,0:T(4,128)(2,1)}, bf16[1,2,6,4]{2,3,1,0:T(4,128)(2,1)}, bf16[1,384,48]{1,2,0:T(8,128)(2,1)}, bf16[1,384...) async-done(((bf16[1,2,6,4]{2,3,1,0:T(4,128)(2,1)}, ...) | async-done | bytes 75472 | tf_op jit(solution)/shard_map/psum | solution.py:297
  1427.8 43.0 %all-reduce.42.cloned.1.call-done = (bf16[1,3,48,384]{3,1,2,0:T(4,128)(2,1)}, bf16[1,3,48,384]{3,1,2,0:T(4,128)(2,1)}, bf16[1,48,1536]{2,1,0:T(8,128)(2,1)}, bf1...) async-done(((bf16[1,3,48,384]{3,1,2,0:T(4,128)(2,1)}, bf16[1,3,48,384]{3,1,2,0:T(4,128)(2,1)}, bf16[1,48,1536]{2,1,0:T(8,128)(2,1)}, ...) | async-done | bytes 811024 | tf_op jit(solution)/shard_map/psum | solution.py:291
  (437 shorter events, 123.0 us)
Async XLA Ops:
  7.2 29.1 %copy-start.98 = (bf16[2,2,48]{2,1,0:T(2,128)(2,1)S(1)}, bf16[2,2,48]{2,1,0:T(2,128)(2,1)}, u32[]{:S(2)}) copy-start(bf16[2,2,48]{2,1,0:T(2,128)(2,1)} %param.19) | copy-start | bytes 1156
  7.2 53.6 %copy-start.103 = (s32[2,128]{1,0:T(2,128)S(1)}, s32[2,128]{1,0:T(2,128)}, u32[]{:S(2)}) copy-start(s32[2,128]{1,0:T(2,128)} %param.12) | copy-start | bytes 3076
  7.2 53.6 %copy-start.91 = (bf16[2,2,6,4]{2,3,1,0:T(4,128)(2,1)S(1)}, bf16[2,2,6,4]{2,3,1,0:T(4,128)(2,1)}, u32[]{:S(2)}) copy-start(bf16[2,2,6,4]{2,3,1,0:T(4,128)(2,1)} %param.14) | copy-start | bytes 580
  7.2 75.7 %copy-start = (f32[2,128,768]{2,1,0:T(8,128)S(1)}, f32[2,128,768]{2,1,0:T(8,128)}, u32[]{:S(2)}) copy-start(f32[2,128,768]{2,1,0:T(8,128)} %param.11) | copy-start | bytes 2359300
  7.2 126.0 %all-gather.27.cloned.1.call-start = ((), (), s32[]{:S(2)}) async-start(), calls=%async_computation.24 | async-start | bytes 1880064 | tf_op jit(solution)/shard_map/all_gather | solution.py:77
  9.0 84.1 %copy-start.46 = (bf16[2,384,48]{1,2,0:T(8,128)(2,1)S(1)}, bf16[2,384,48]{1,2,0:T(8,128)(2,1)}, u32[]{:S(2)}) copy-start(bf16[2,384,48]{1,2,0:T(8,128)(2,1)} %param.15) | copy-start | bytes 221188
  9.0 190.7 %all-reduce.26.cloned.1.call-start = ((), (), s32[]{:S(2)}) async-start(), calls=%async_computation.10 | async-start | bytes 1572864 | tf_op jit(solution)/shard_map/psum | solution.py:133
  82.8 71.6 %copy-start.56 = (f32[6,64]{1,0:T(8,128)}, f32[6,64]{1,0:T(8,128)S(1)}, u32[]{:S(2)}) copy-start(f32[6,64]{1,0:T(8,128)S(1)} %copy.213) | copy-start | bytes 4612
  117.0 57.7 %copy-start.12 = (bf16[1,384,768]{1,2,0:T(8,128)(2,1)}, bf16[1,384,768]{1,2,0:T(8,128)(2,1)S(1)}, u32[]{:S(2)}) copy-start(bf16[1,384,768]{1,2,0:T(8,128)(2,1)S(1)} %all-gather.5) | copy-start | bytes 1769476
  117.0 18.5 %copy-start.51 = (f32[2,128]{1,0:T(2,128)}, f32[2,128]{1,0:T(2,128)S(1)}, u32[]{:S(2)}) copy-start(f32[2,128]{1,0:T(2,128)S(1)} %broadcast_multiply_fusion.11) | copy-start | bytes 3076
  121.8 13.7 copy-start.59
  122.1 49.4 %copy-start.22 = (pred[2,128,512]{2,1,0:T(8,128)(4,1)}, pred[2,128,512]{2,1,0:T(8,128)(4,1)S(1)}, u32[]{:S(2)}) copy-start(pred[2,128,512]{2,1,0:T(8,128)(4,1)S(1)} %compare_and_fusion) | copy-start | bytes 393220
  133.2 115.2 %copy-start.68 = (f32[768]{0:T(1024)}, f32[768]{0:T(1024)S(1)}, u32[]{:S(2)}) copy-start(f32[768]{0:T(1024)S(1)} %get-tuple-element.49) | copy-start | bytes 9220
  157.9 13.7 copy-start.85
  176.1 72.3 %all-gather.29.cloned.1.call-start = ((), (), s32[]{:S(2)}) async-start(), calls=%async_computation.25 | async-start | bytes 2506752 | tf_op jit(solution)/shard_map/all_gather | solution.py:80
  176.9 119.4 %all-gather.31.cloned.1.call-start = ((), (), s32[]{:S(2)}) async-start(), calls=%async_computation.26 | async-start | bytes 2506752 | tf_op jit(solution)/shard_map/all_gather | solution.py:82
  177.7 233.5 %all-reduce.28.cloned.1.call-start = ((), (), s32[]{:S(2)}) async-start(), calls=%async_computation.11 | async-start | bytes 1572864 | tf_op jit(solution)/shard_map/psum | solution.py:143
  201.1 49.8 %copy-start.61 = (f32[2,128]{1,0:T(2,128)}, f32[2,128]{1,0:T(2,128)S(1)}, u32[]{:S(2)}) copy-start(f32[2,128]{1,0:T(2,128)S(1)} %broadcast_multiply_fusion.10) | copy-start | bytes 3076
  201.3 49.6 %copy-start.73 = (f32[2,128]{1,0:T(2,128)}, f32[2,128]{1,0:T(2,128)S(1)}, u32[]{:S(2)}) copy-start(f32[2,128]{1,0:T(2,128)S(1)} %add_rsqrt_fusion.2) | copy-start | bytes 3076
  250.9 45.3 %copy-start.105 = (f32[2,128,1536]{2,1,0:T(8,128)}, f32[2,128,1536]{2,1,0:T(8,128)S(1)}, u32[]{:S(2)}) copy-start(f32[2,128,1536]{2,1,0:T(8,128)S(1)} %convolution_add_fusion.1) | copy-start | bytes 4718596
  250.9 49.6 %copy-start.94 = (bf16[1,4,48]{2,1,0:T(4,128)(2,1)S(1)}, bf16[1,4,48]{2,1,0:T(4,128)(2,1)}, u32[]{:S(2)}) copy-start(bf16[1,4,48]{2,1,0:T(4,128)(2,1)} %get-tuple-element.115) | copy-start | bytes 1156
  299.9 24.5 %copy-start.97 = (bf16[1,2,48]{2,1,0:T(2,128)(2,1)S(1)}, bf16[1,2,48]{2,1,0:T(2,128)(2,1)}, u32[]{:S(2)}) copy-start(bf16[1,2,48]{2,1,0:T(2,128)(2,1)} %get-tuple-element.116) | copy-start | bytes 580
  299.9 47.4 %copy-start.89 = (bf16[1,2,6,4]{2,3,1,0:T(4,128)(2,1)S(1)}, bf16[1,2,6,4]{2,3,1,0:T(4,128)(2,1)}, u32[]{:S(2)}) copy-start(bf16[1,2,6,4]{2,3,1,0:T(4,128)(2,1)} %get-tuple-element.110) | copy-start | bytes 292
  299.9 112.8 %all-gather.33.cloned.1.call-start = ((), (), s32[]{:S(2)}) async-start(), calls=%async_computation.27 | async-start | bytes 1880064 | tf_op jit(solution)/shard_map/all_gather | solution.py:77
  300.5 181.9 %all-reduce.30.cloned.1.call-start = ((), (), s32[]{:S(2)}) async-start(), calls=%async_computation.12 | async-start | bytes 1572864 | tf_op jit(solution)/shard_map/psum | solution.py:133
  437.3 15.7 %copy-start.24 = (pred[2,128,512]{2,1,0:T(8,128)(4,1)S(1)}, pred[2,128,512]{2,1,0:T(8,128)(4,1)}, u32[]{:S(2)}) copy-start(pred[2,128,512]{2,1,0:T(8,128)(4,1)} %copy-done.22) | copy-start | bytes 393220
  437.3 18.9 %copy-start.87 = (f32[2,6,128]{2,1,0:T(8,128)}, f32[2,6,128]{2,1,0:T(8,128)S(1)}, u32[]{:S(2)}) copy-start(f32[2,6,128]{2,1,0:T(8,128)S(1)} %log_add_fusion) | copy-start | bytes 18436
  456.2 26.2 %copy-start.72 = (f32[768]{0:T(1024)S(1)}, f32[768]{0:T(1024)}, u32[]{:S(2)}) copy-start(f32[768]{0:T(1024)} %get-tuple-element.44) | copy-start | bytes 9220
  458.2 72.4 %all-gather.35.cloned.1.call-start = ((), (), s32[]{:S(2)}) async-start(), calls=%async_computation.28 | async-start | bytes 2506752 | tf_op jit(solution)/shard_map/all_gather | solution.py:80
  458.2 72.3 %copy-start.70 = (f32[768]{0:T(1024)S(1)}, f32[768]{0:T(1024)}, u32[]{:S(2)}) copy-start(f32[768]{0:T(1024)} %get-tuple-element.43) | copy-start | bytes 9220
  458.9 119.1 %all-gather.37.cloned.1.call-start = ((), (), s32[]{:S(2)}) async-start(), calls=%async_computation.29 | async-start | bytes 2506752 | tf_op jit(solution)/shard_map/all_gather | solution.py:82
  459.7 146.7 %all-reduce.32.cloned.1.call-start = ((), (), s32[]{:S(2)}) async-start(), calls=%async_computation.13 | async-start | bytes 1572864 | tf_op jit(solution)/shard_map/psum | solution.py:143
  483.7 50.5 %copy-start.66 = (f32[2,128]{1,0:T(2,128)}, f32[2,128]{1,0:T(2,128)S(1)}, u32[]{:S(2)}) copy-start(f32[2,128]{1,0:T(2,128)S(1)} %broadcast_multiply_fusion.8) | copy-start | bytes 3076
  484.0 50.3 %copy-start.75 = (f32[2,128]{1,0:T(2,128)}, f32[2,128]{1,0:T(2,128)S(1)}, u32[]{:S(2)}) copy-start(f32[2,128]{1,0:T(2,128)S(1)} %add_rsqrt_fusion) | copy-start | bytes 3076
  582.1 64.5 %reduce-scatter.21.cloned.1.call-start = ((), (), s32[]{:S(2)}) async-start(), calls=%async_computation.14 | async-start | bytes 983040 | tf_op jit(solution)/shard_map/reduce_scatter | solution.py:257
  609.6 4.7 copy-start.25
  609.6 4.7 copy-start.88
  622.7 48.5 %reduce-scatter.23.cloned.1.call-start = ((), (), s32[]{:S(2)}) async-start(), calls=%async_computation.15 | async-start | bytes 983040 | tf_op jit(solution)/shard_map/reduce_scatter | solution.py:260
  628.8 69.4 %all-reduce.34.cloned.1.call-start = ((), (), s32[]{:S(2)}) async-start(), calls=%async_computation.16 | async-start | bytes 786432 | tf_op jit(solution)/shard_map/psum | solution.py:274
  632.0 42.3 %copy-start.44 = (bf16[1,2,128,384]{3,2,0,1:T(8,128)(2,1)}, bf16[1,2,128,384]{3,2,0,1:T(8,128)(2,1)S(1)}, u32[]{:S(2)}) copy-start(bf16[1,2,128,384]{3,2,0,1:T(8,128)(2,1)S(1)} %copy.236) | copy-start | bytes 589828
  671.1 27.1 %copy-start.54 = (f32[2,128]{1,0:T(2,128)S(1)}, f32[2,128]{1,0:T(2,128)}, u32[]{:S(2)}) copy-start(f32[2,128]{1,0:T(2,128)} %copy-done.53) | copy-start | bytes 3076
  671.1 27.1 %copy-start.64 = (f32[2,128]{1,0:T(2,128)S(1)}, f32[2,128]{1,0:T(2,128)}, u32[]{:S(2)}) copy-start(f32[2,128]{1,0:T(2,128)} %copy-done.63) | copy-start | bytes 3076
  674.3 75.6 %reduce-scatter.25.cloned.1.call-start = ((), (), s32[]{:S(2)}) async-start(), calls=%async_computation.17 | async-start | bytes 983040 | tf_op jit(solution)/shard_map/reduce_scatter | solution.py:257
  717.6 4.7 copy-start.18
  717.6 4.7 copy-start.57
  726.0 48.6 %reduce-scatter.27.cloned.1.call-start = ((), (), s32[]{:S(2)}) async-start(), calls=%async_computation.18 | async-start | bytes 983040 | tf_op jit(solution)/shard_map/reduce_scatter | solution.py:260
  732.5 86.0 %all-reduce.36.cloned.1.call-start = ((), (), s32[]{:S(2)}) async-start(), calls=%async_computation.19 | async-start | bytes 786432 | tf_op jit(solution)/shard_map/psum | solution.py:274
  777.8 124.1 %reduce-scatter.39.cloned.1.call-start = ((), (), s32[]{:S(2)}) async-start(), calls=%async_computation.31 | async-start | bytes 626688
  780.4 173.1 %reduce-scatter.37.cloned.1.call-start = ((), (), s32[]{:S(2)}) async-start(), calls=%async_computation.30 | async-start | bytes 626688
  782.8 281.8 %all-reduce.38.cloned.1.call-start = ((), (), s32[]{:S(2)}) async-start(), calls=%async_computation.32 | async-start | bytes 9437184
  786.0 5.3 copy-start.43
  786.0 5.3 copy-start.45
  786.0 5.3 copy-start.48
  786.0 5.3 copy-start.52
  786.0 5.3 copy-start.60
  786.0 5.3 copy-start.102
  798.6 344.3 %reduce-scatter.31.cloned.1.call-start = ((), (), s32[]{:S(2)}) async-start(), calls=%async_computation.21 | async-start | bytes 2506752 | tf_op jit(solution)/shard_map/reduce_scatter | solution.py:310
  802.1 418.8 %reduce-scatter.35.cloned.1.call-start = ((), (), s32[]{:S(2)}) async-start(), calls=%async_computation.23 | async-start | bytes 2506752 | tf_op jit(solution)/shard_map/reduce_scatter | solution.py:322
  807.1 491.7 %reduce-scatter.29.cloned.1.call-start = ((), (), s32[]{:S(2)}) async-start(), calls=%async_computation.20 | async-start | bytes 2506752 | tf_op jit(solution)/shard_map/reduce_scatter | solution.py:310
  810.6 566.0 %reduce-scatter.33.cloned.1.call-start = ((), (), s32[]{:S(2)}) async-start(), calls=%async_computation.22 | async-start | bytes 2506752 | tf_op jit(solution)/shard_map/reduce_scatter | solution.py:322
  814.8 606.4 %all-reduce.40.cloned.1.call-start = ((), (), s32[]{:S(2)}) async-start(), calls=%async_computation.33 | async-start | bytes 165888 | tf_op jit(solution)/shard_map/psum | solution.py:297
  818.3 558.3 %copy-start.4 = (f32[2,128,768]{2,1,0:T(8,128)S(1)}, f32[2,128,768]{2,1,0:T(8,128)}, u32[]{:S(2)}) copy-start(f32[2,128,768]{2,1,0:T(8,128)} %copy-done.3) | copy-start | bytes 2359300
  818.6 558.1 %copy-start.21 = (bf16[2,128,768]{2,1,0:T(8,128)(2,1)S(1)}, bf16[2,128,768]{2,1,0:T(8,128)(2,1)}, u32[]{:S(2)}) copy-start(bf16[2,128,768]{2,1,0:T(8,128)(2,1)} %all-reduce.36.cloned.1.call-done) | copy-start | bytes 1179652
  953.5 517.3 %all-reduce.42.cloned.1.call-start = ((), (), s32[]{:S(2)}) async-start(), calls=%async_computation.34 | async-start | bytes 1769472 | tf_op jit(solution)/shard_map/psum | solution.py:291
  (69 other events, 173.2 us)
Sparse Core Ops, SparseCore 0:
  10.8 47.1 all-gather.26
  176.2 21.9 all-reduce.25
  201.2 47.1 all-gather.28
  251.2 45.0 all-gather.30
  300.0 24.0 all-reduce.27
  326.1 46.5 all-gather.32
  458.3 22.0 all-reduce.29
  483.4 47.1 all-gather.34
  532.9 45.0 all-gather.36
  582.3 24.0 all-reduce.31
  622.8 23.7 reduce-scatter.20
  648.9 22.2 reduce-scatter.22
  674.5 23.7 all-reduce.33
  726.1 23.8 reduce-scatter.24
  752.3 22.1 reduce-scatter.26
  777.9 23.7 all-reduce.35
  805.3 73.3 reduce-scatter.38
  882.3 71.1 reduce-scatter.36
  956.9 107.6 all-reduce.37
  1068.2 74.6 reduce-scatter.30
  1146.6 74.2 reduce-scatter.34
  1224.6 74.1 reduce-scatter.28
  1302.5 74.1 reduce-scatter.32
  1381.0 40.2 all-reduce.39
  1424.5 46.2 all-reduce.41
